TPU v7x, 128 devices: a whole 4x4x4 slice. The times are simulated.
128 devices in a mesh: pop: 8 (over y_lo, x), col: 16 (over z, y_hi, core).
Axes of the slice: x: 4, y: 4 (y_hi: 2, y_lo: 2; y = y_hi * 2 + y_lo), z: 4, core: 2. Of those that a mesh axis runs over, the one named last changes fastest.
Arguments:
- acts: bfloat16 [128, 64, 3584], P('pop', None, 'col'), may hold values from -6 to 6
- weight: bfloat16 [3584, 18944], P('pop', 'col'), may hold values from -0.09375 to 0.09375
- input_noise_factor: bfloat16 [128, 4, 3584], P('pop'), may hold values from -1 to 1
- output_noise_factor: bfloat16 [128, 4, 18944], P('pop', None, 'col'), may hold values from -8 to 8
- ranks: int32 [128], P('pop'), may hold values from 0 to 127, each once
Outputs:
- member_out: bfloat16 [128, 64, 18944], P('pop', None, 'col')
- step_dir: float32 [3584, 18944], P('pop', 'col')
- new_weight: bfloat16 [3584, 18944], P('pop', 'col')
Inputs may be any that keep to these rules, and one draw needn't show every extreme that they name: `ranks`: every member has a different rank.
All inputs are finite; a program needn't handle non-finite values.
Results may differ from a plain program's by a relative error of at most 0.0034.
Values may be sent and summed in bfloat16 or wider, within the bound.
A program may use at most 192 MiB of HBM per device.

v0:
```python
import jax
import jax.numpy as jnp
from jax import lax
from jax.sharding import PartitionSpec as P

D = 3584
F = 18944


def body(acts, weight, input_noise_factor, output_noise_factor, ranks):
    whole = lax.all_gather(acts, "col", axis=2, tiled=True)
    members, tokens, width = whole.shape
    flat = whole.reshape(members * tokens, width)
    base = jnp.dot(
        flat, lax.all_gather(weight, "pop", axis=0, tiled=True), preferred_element_type=jnp.float32
    )
    lower_bound = jnp.einsum(
        "mtd,mrd->mtr", whole, input_noise_factor, preferred_element_type=jnp.float32
    )
    pert = jnp.einsum(
        "zlh,zhj->zlj",
        lower_bound,
        output_noise_factor.astype(jnp.float32),
        precision=lax.Precision.HIGHEST,
    )
    member_out = (base.reshape(members, tokens, -1) + 0.5 * pert).astype(jnp.bfloat16)
    pop_count = lax.axis_size("pop")
    total_members = ranks.shape[0] * pop_count
    fit = ranks.astype(jnp.float32) / (total_members - 1) - 0.5
    scaled_update = (output_noise_factor.astype(jnp.float32) * fit[:, None, None]).astype(
        jnp.bfloat16
    )
    weight_change = lax.psum_scatter(
        jnp.einsum(
            "vjs,vjg->sg", input_noise_factor, scaled_update, preferred_element_type=jnp.float32
        ),
        "pop",
        scatter_dimension=0,
        tiled=True,
    )
    mean_sq = lax.psum(jnp.sum(weight_change * weight_change), ("pop", "col")) / (D * F)
    step_dir = weight_change * lax.rsqrt(mean_sq + 1e-06)
    new_weight = (weight.astype(jnp.float32) + 0.01 * step_dir).astype(jnp.bfloat16)
    return (member_out, step_dir, new_weight)


def solution(mesh):
    in_specs = (
        P("pop", None, "col"),
        P("pop", "col"),
        P("pop", None, None),
        P("pop", None, "col"),
        P("pop"),
    )
    out_specs = (P("pop", None, "col"), P("pop", "col"), P("pop", "col"))
    return jax.shard_map(body, mesh=mesh, in_specs=in_specs, out_specs=out_specs, check_vma=False)
```

profile of v0, /device:TPU:1, one launch (start us, length us, event | category | flops | bytes accessed | tf_op | source)
XLA Modules:
  0.0 489.5 jit_solution(12580459237026647606)
XLA Ops:
  7.2 0.0 copy-start
  7.2 0.0 all-gather.3.cloned.1.call-start
  7.2 2.7 copy.13
  10.0 0.0 all-gather.3.cloned.1.call-update
  10.0 0.0 all-gather.5.cloned.1.call-start
  10.0 0.7 all-gather.5.cloned.1.call-update
  10.7 0.0 reduce-scatter.4.cloned.1.call-start
  10.8 0.7 multiply_add_fusion
  11.4 1.0 multiply_convert_fusion
  12.5 0.0 copy-done
  12.5 8.2 %convolution_bitcast_fusion = f32[3584,1184]{0,1:T(8,128)} fusion(bf16[16,4,3584]{2,1,0:T(4,128)(2,1)S(1)} %copy-done, bf16[16,4,1184]{2,1,0:T(4,128)(2,1)S(1)} %multiply_convert_fusion), kind=kOutput, calls=%fused_computation | convolution fusion | flops 543162368 | bytes 17584128 | tf_op jit(solution)/shard_map/vjs,vjg->sg/dot_general | solution.py:34
  20.7 19.0 %copy.20 = f32[3584,1184]{1,0:T(8,128)} copy(f32[3584,1184]{0,1:T(8,128)} %convolution_bitcast_fusion) | data formatting | bytes 33947648
  39.7 0.0 copy-start.3
  39.7 0.0 reduce-scatter.4.cloned.1.call-update
  39.7 1.2 copy-done.3
  41.0 1.5 copy.17
  42.5 71.7 %all-gather.3.cloned.1.call-done = bf16[16,64,3584]{1,0,2:T(8,128)(2,1)} async-done(((bf16[16,64,224]{1,0,2:T(8,128)(2,1)}), bf16[16,64,3584]{1,0,2:T(8,128)(2,1)}) %all-gather.3.cloned.1.call-update) | async-done | bytes 7340048 | tf_op jit(solution)/shard_map/all_gather | solution.py:11
  114.2 16.3 %copy.14 = bf16[16,64,3584]{2,1,0:T(8,128)(2,1)} copy(bf16[16,64,3584]{1,0,2:T(8,128)(2,1)} %all-gather.3.cloned.1.call-done) | data formatting | bytes 14680064 | tf_op jit(solution)/shard_map/all_gather | solution.py:11
  130.4 5.1 %fusion.4 = f32[16,64,4]{1,2,0:T(4,128)S(1)} fusion(bf16[16,64,3584]{2,1,0:T(8,128)(2,1)} %copy.14, bf16[16,4,3584]{2,1,0:T(4,128)(2,1)S(1)} %copy-done), kind=kOutput, calls=%fused_computation.11 | convolution fusion | flops 29360128 | bytes 7815168 | tf_op jit(solution)/shard_map/mtd,mrd->mtr/dot_general | solution.py:17
  135.5 76.5 %all-gather.5.cloned.1.call-done = bf16[3584,1184]{1,0:T(8,128)(2,1)} async-done(((bf16[448,1184]{1,0:T(8,128)(2,1)}), bf16[3584,1184]{1,0:T(8,128)(2,1)}) %all-gather.5.cloned.1.call-update) | async-done | bytes 8486928 | tf_op jit(solution)/shard_map/all_gather | solution.py:15
  212.0 16.1 %fusion = f32[16,64,1184]{2,1,0:T(8,128)} fusion(bf16[16,64,3584]{2,1,0:T(8,128)(2,1)} %copy.14, bf16[3584,1184]{1,0:T(8,128)(2,1)} %all-gather.5.cloned.1.call-done), kind=kOutput, calls=%fused_computation.1 | convolution fusion | flops 8690597888 | bytes 20676608 | tf_op jit(solution)/shard_map/dot_general | solution.py:14
  228.1 0.0 copy-start.4
  228.1 171.4 %reduce-scatter.4.cloned.1.call-done = f32[448,1184]{1,0:T(8,128)} async-done(((f32[3584,1184]{1,0:T(8,128)}), f32[448,1184]{1,0:T(8,128)}) %reduce-scatter.4.cloned.1.call-update) | async-done | bytes 2121744
  399.5 2.3 copy.21
  401.8 1.2 multiply_reduce_fusion
  403.0 0.0 copy-done.4
  403.1 6.3 %add_convert_fusion = bf16[16,64,1184]{2,1,0:T(8,128)(2,1)} fusion(f32[16,64,1184]{2,1,0:T(8,128)} %fusion, f32[16,64,4]{1,2,0:T(4,128)S(1)} %fusion.4, bf16[16,4,1184]{2,1,0:T(4,128)(2,1)S(1)} %copy-done.4), kind=kOutput, calls=%fused_computation.3 | convolution fusion | flops 61833216 | bytes 7442432 | tf_op jit(solution)/shard_map/zlh,zhj->zlj/dot_general | solution.py:20
  409.4 64.5 %psum.7 = f32[]{:T(128)} all-reduce(f32[]{:T(128)} %multiply_reduce_fusion), channel_id=1, replica_groups=mesh['pop'=8,'col'=16] {'pop','col'}, use_global_device_ids=true, to_apply=%region_2.0 | all-reduce | flops 1 | bytes 8 | tf_op jit(solution)/shard_map/psum | solution.py:41
  474.6 0.0 copy-start.1
  474.6 3.6 add_convert_fusion.1
  478.2 0.0 copy-start.2
  478.2 3.2 copy.18
  481.4 0.0 copy-done.2
  481.4 1.5 copy.19
  483.0 0.0 copy-done.1
Async XLA Ops:
  7.2 5.3 %copy-start = (bf16[16,4,3584]{2,1,0:T(4,128)(2,1)S(1)}, bf16[16,4,3584]{2,1,0:T(4,128)(2,1)}, u32[]{:S(2)}) copy-start(bf16[16,4,3584]{2,1,0:T(4,128)(2,1)} %param.7) | copy-start | bytes 1376260
  7.2 107.0 %all-gather.3.cloned.1.call-start = ((), (), s32[]{:S(2)}) async-start(), calls=%async_computation.1 | async-start | bytes 15597568 | tf_op jit(solution)/shard_map/all_gather | solution.py:11
  10.0 202.0 %all-gather.5.cloned.1.call-start = ((), (), s32[]{:S(2)}) async-start(), calls=%async_computation.2 | async-start | bytes 10321920 | tf_op jit(solution)/shard_map/all_gather | solution.py:15
  10.7 388.8 %reduce-scatter.4.cloned.1.call-start = ((), (), s32[]{:S(2)}) async-start(), calls=%async_computation.3 | async-start | bytes 20643840
  39.7 1.3 copy-start.3
  228.1 175.0 %copy-start.4 = (bf16[16,4,1184]{2,1,0:T(4,128)(2,1)S(1)}, bf16[16,4,1184]{2,1,0:T(4,128)(2,1)}, u32[]{:S(2)}) copy-start(bf16[16,4,1184]{2,1,0:T(4,128)(2,1)} %param.8) | copy-start | bytes 454660
  474.6 8.4 %copy-start.1 = (bf16[16,4,3584]{2,1,0:T(4,128)(2,1)S(1)}, bf16[16,4,3584]{2,1,0:T(4,128)(2,1)}, u32[]{:S(2)}) copy-start(bf16[16,4,3584]{2,1,0:T(4,128)(2,1)} %param.7) | copy-start | bytes 1376260
  478.2 3.2 copy-start.2
Sparse Core Ops, SparseCore 0:
  11.0 103.0 all-gather.2
  115.8 96.1 all-gather.4
  214.5 184.9 reduce-scatter.3
where the time goes:
time: 491 us; the launch traced here: 489 us
  waiting for transfers between devices  320 us (65%)
  blocking collectives  64.5 us (13%)
  local copies, waits for them, and re-layouts  47.8 us (10%)
  matrix products  35.7 us (7%)
  between operations  14.5 us (3%)
  other arithmetic  6.53 us (1%)
    unnamed x4, waiting for transfers between devices  172 us
    all_gather x1, waiting for transfers between devices, body(): lax.all_gather(weight, 'pop', axis=0, tiled=True)  76.5 us
    all_gather x1, waiting for transfers between devices, body(): whole = lax.all_gather(acts, 'col', axis=2, tiled=True)  71.7 us
    psum x1, blocking collectives, body(): lax.psum(jnp.sum(weight_change * weight_change), ('pop', 'col')) / (D * F)  64.5 us
    unnamed x16, local copies, waits for them, and re-layouts  31.5 us
    all_gather x1, local copies, waits for them, and re-layouts, body(): whole = lax.all_gather(acts, 'col', axis=2, tiled=True)  16.3 us
    dot_general x1, matrix products, body(): jnp.dot(flat, lax.all_gather(weight, 'pop', axis=0, tiled=True), preferre...  16.1 us
  transfers between devices with their start and end apart: 3, of which 3 were waited for; matrix products, arithmetic and copies ran while one was open for 14% of the time, Pallas kernels for 0%

commit v1 on v0

--- a/solution.py
+++ b/solution.py
@@ -8,7 +8,9 @@
 
 
 def body(acts, weight, input_noise_factor, output_noise_factor, ranks):
-    whole = lax.all_gather(acts, "col", axis=2, tiled=True)
+    whole = jnp.concatenate(
+        lax.all_to_all(jnp.stack([acts] * lax.axis_size("col")), "col", 0, 0), axis=2
+    )
     members, tokens, width = whole.shape
     flat = whole.reshape(members * tokens, width)
     base = jnp.dot(

time: 491 us -> 518 us (1.055)
  local copies, waits for them, and re-layouts: 47.8 us -> 61.9 us
  starting transfers between devices: 0.12 us -> 9.68 us
    all_to_all x0 -> x1, waiting for transfers between devices: none -> 324 us  [body(): lax.all_to_all(jnp.stack([acts] * lax.axis_size('col')), 'col', 0, 0)]
    unnamed x4 -> x3, waiting for transfers between devices: 172 us -> 0.7 us
    all_gather x1, waiting for transfers between devices: 76.5 us -> 0.01 us  [body(): lax.all_gather(weight, 'pop', axis=0, tiled=True)]
    all_gather x1 -> x0, waiting for transfers between devices: 71.7 us -> none  [body(): whole = lax.all_gather(acts, 'col', axis=2, tiled=True)]
    dot_general x0 -> x1, local copies, waits for them, and re-layouts: none -> 16.6 us  [body(): jnp.dot(flat, lax.all_gather(weight, 'pop', axis=0, tiled=True), preferre...]
    all_gather x1 -> x0, local copies, waits for them, and re-layouts: 16.3 us -> none  [body(): whole = lax.all_gather(acts, 'col', axis=2, tiled=True)]
    reshape x0 -> x1, local copies, waits for them, and re-layouts: none -> 12.4 us  [body(): jnp.concatenate(lax.all_to_all(jnp.stack([acts] * lax.axis_size('col')),...]
    all_to_all x0 -> x1, starting transfers between devices: none -> 9.61 us  [body(): lax.all_to_all(jnp.stack([acts] * lax.axis_size('col')), 'col', 0, 0)]
  transfers between devices with their start and end apart: 3 -> 3, of which waited for: 3 -> 1; matrix products, arithmetic and copies ran while one was open for 14% -> 16% of each run, Pallas kernels for 0% -> 0%
where the time goes in v1:
time: 518 us; the launch traced here: 516 us
  waiting for transfers between devices  325 us (63%)
  blocking collectives  62.8 us (12%)
  local copies, waits for them, and re-layouts  61.9 us (12%)
  matrix products  35.6 us (7%)
  between operations  14.8 us (3%)
  starting transfers between devices  9.68 us (2%)
  other arithmetic  6.48 us (1%)
    all_to_all x1, waiting for transfers between devices, body(): lax.all_to_all(jnp.stack([acts] * lax.axis_size('col')), 'col', 0, 0)  324 us
    psum x1, blocking collectives, body(): lax.psum(jnp.sum(weight_change * weight_change), ('pop', 'col')) / (D * F)  62.8 us
    unnamed x15, local copies, waits for them, and re-layouts  28.5 us
    dot_general x1, local copies, waits for them, and re-layouts, body(): jnp.dot(flat, lax.all_gather(weight, 'pop', axis=0, tiled=True), preferre...  16.6 us
    dot_general x1, matrix products, body(): jnp.dot(flat, lax.all_gather(weight, 'pop', axis=0, tiled=True), preferre...  16.1 us
    reshape x1, local copies, waits for them, and re-layouts, body(): jnp.concatenate(lax.all_to_all(jnp.stack([acts] * lax.axis_size('col')),...  12.4 us
  transfers between devices with their start and end apart: 3, of which 1 were waited for; matrix products, arithmetic and copies ran while one was open for 16% of the time, Pallas kernels for 0%

profile of v1, /device:TPU:1, one launch (start us, length us, event | category | flops | bytes accessed | tf_op | source)
XLA Modules:
  0.0 516.3 jit_solution(10278297098495772513)
XLA Ops:
  7.2 0.0 copy-start
  7.2 0.0 all-gather.2.cloned.1.call-start
  7.2 0.7 all-gather.2.cloned.1.call-update
  7.9 0.0 reduce-scatter.4.cloned.1.call-start
  8.0 0.7 multiply_add_fusion
  8.6 1.0 multiply_convert_fusion
  9.7 0.0 copy-done
  9.7 8.2 %convolution_bitcast_fusion = f32[3584,1184]{0,1:T(8,128)} fusion(bf16[16,4,3584]{2,1,0:T(4,128)(2,1)S(1)} %copy-done, bf16[16,4,1184]{2,1,0:T(4,128)(2,1)S(1)} %multiply_convert_fusion), kind=kOutput, calls=%fused_computation | convolution fusion | flops 543162368 | bytes 17584128 | tf_op jit(solution)/shard_map/vjs,vjg->sg/dot_general | solution.py:36
  17.9 18.9 %copy.19 = f32[3584,1184]{1,0:T(8,128)} copy(f32[3584,1184]{0,1:T(8,128)} %convolution_bitcast_fusion) | data formatting | bytes 33947648
  36.7 0.0 copy-start.4
  36.7 0.0 reduce-scatter.4.cloned.1.call-update
  36.8 1.0 copy-done.4
  37.8 4.4 stack.2
  42.1 0.0 copy-start.2
  42.1 9.6 %all-to-all-start = ((bf16[16,16,64,224]{3,2,1,0:T(8,128)(2,1)}), bf16[16,16,64,224]{3,2,1,0:T(8,128)(2,1)}, u32[]{:S(2)}, u32[]{:S(2)}) async-start(bf16[16,16,64,224]{3,2,1,0:T(8,128)(2,1)} %stack.2), calls=%async_computation | async-start | bytes 16777216 | tf_op jit(solution)/shard_map/all_to_all | solution.py:12
  51.7 0.0 copy-done.2
  51.8 1.5 copy.16
  53.3 324.4 %all-to-all-done = bf16[16,16,64,224]{3,2,1,0:T(8,128)(2,1)} async-done(((bf16[16,16,64,224]{3,2,1,0:T(8,128)(2,1)}), bf16[16,16,64,224]{3,2,1,0:T(8,128)(2,1)}, u32[]{:S(2)}, u32[]{:S(2)}) %all-to-all-start) | async-done | bytes 7340064 | tf_op jit(solution)/shard_map/all_to_all | solution.py:12
  377.6 12.4 %copy.13 = bf16[16,64,16,224]{3,2,1,0:T(8,128)(2,1)} copy(bf16[16,64,16,224]{3,1,0,2:T(8,128)(2,1)} %bitcast) | data formatting | bytes 14680064 | tf_op jit(solution)/shard_map/reshape | solution.py:11
  390.0 16.6 %dot_general.16 = bf16[16,64,3584]{2,1,0:T(8,128)(2,1)} reshape(bf16[16,64,16,224]{3,2,1,0:T(8,128)(2,1)} %copy.13) | data formatting | bytes 14680064 | tf_op jit(solution)/shard_map/dot_general | solution.py:16
  406.6 5.1 fusion.4
  411.7 0.0 all-gather.2.cloned.1.call-done
  411.7 16.1 %fusion = f32[16,64,1184]{2,1,0:T(8,128)} fusion(bf16[16,64,3584]{2,1,0:T(8,128)(2,1)} %dot_general.16, bf16[3584,1184]{1,0:T(8,128)(2,1)} %all-gather.2.cloned.1.call-done), kind=kOutput, calls=%fused_computation.1 | convolution fusion | flops 8690597888 | bytes 20676608 | tf_op jit(solution)/shard_map/dot_general | solution.py:16
  427.8 0.0 copy-start.3
  427.8 0.0 reduce-scatter.4.cloned.1.call-done
  427.8 2.3 copy.20
  430.1 1.2 multiply_reduce_fusion
  431.3 0.0 copy-done.3
  431.3 6.3 %add_convert_fusion = bf16[16,64,1184]{2,1,0:T(8,128)(2,1)} fusion(f32[16,64,1184]{2,1,0:T(8,128)} %fusion, f32[16,64,4]{1,2,0:T(4,128)S(1)} %fusion.4, bf16[16,4,1184]{2,1,0:T(4,128)(2,1)S(1)} %copy-done.3), kind=kOutput, calls=%fused_computation.3 | convolution fusion | flops 61833216 | bytes 7442432 | tf_op jit(solution)/shard_map/zlh,zhj->zlj/dot_general | solution.py:22
  437.6 62.8 %psum.7 = f32[]{:T(128)} all-reduce(f32[]{:T(128)} %multiply_reduce_fusion), channel_id=1, replica_groups=mesh['pop'=8,'col'=16] {'pop','col'}, use_global_device_ids=true, to_apply=%region_2.0 | all-reduce | flops 1 | bytes 8 | tf_op jit(solution)/shard_map/psum | solution.py:43
  501.1 3.6 add_convert_fusion.1
  504.7 0.0 copy-start.1
  504.7 3.2 copy.17
  507.9 0.0 copy-done.1
  507.9 1.5 copy.18
Async XLA Ops:
  7.2 2.5 copy-start
  7.2 404.5 %all-gather.2.cloned.1.call-start = ((), (), s32[]{:S(2)}) async-start(), calls=%async_computation.2 | async-start | bytes 10321920 | tf_op jit(solution)/shard_map/all_gather | solution.py:17
  7.9 419.9 %reduce-scatter.4.cloned.1.call-start = ((), (), s32[]{:S(2)}) async-start(), calls=%async_computation.3 | async-start | bytes 20643840
  36.7 1.0 copy-start.4
  42.1 9.6 %copy-start.2 = (bf16[448,1184]{1,0:T(8,128)(2,1)S(1)}, bf16[448,1184]{1,0:T(8,128)(2,1)}, u32[]{:S(2)}) copy-start(bf16[448,1184]{1,0:T(8,128)(2,1)} %param.6) | copy-start | bytes 3182596
  42.1 335.5 %all-to-all-start = ((bf16[16,16,64,224]{3,2,1,0:T(8,128)(2,1)}), bf16[16,16,64,224]{3,2,1,0:T(8,128)(2,1)}, u32[]{:S(2)}, u32[]{:S(2)}) async-start(bf16[16,16,64,224]{3,2,1,0:T(8,128)(2,1)} %stack.2), calls=%async_computation | async-start | bytes 16777216 | tf_op jit(solution)/shard_map/all_to_all | solution.py:12
  427.8 3.6 copy-start.3
  504.7 3.2 copy-start.1
Sparse Core Ops, SparseCore 0:
  9.6 102.2 all-gather.1
  114.4 184.9 reduce-scatter.3
